TPU v7x, 512 devices: a whole 4x4x16 slice. The times are simulated.
512 devices in a mesh: row: 32 (over y, x, core), col: 16 (over z).
Axes of the slice: x: 4, y: 4, z: 16, core: 2. Of those that a mesh axis runs over, the one named last changes fastest.
Arguments:
- kernel: bfloat16 [16, 32, 16, 16, 512], P(None, 'row', None, 'col'), as said below
Outputs:
- factor: float32 [16, 32, 16, 16, 512], P(None, 'row', None, 'col')
Inputs may be any that keep to these rules, and one draw needn't show every extreme that they name: kernel holds a symmetric positive definite matrix.
All inputs are finite; a program needn't handle non-finite values.
Results may differ from a plain program's by a relative error of at most 0.0046.
Values may be sent and summed in bfloat16 or wider, within the bound.
A program may use at most 64 MiB of HBM per device.

v0:
```python
import jax
import jax.numpy as jnp
from jax import lax
from jax.sharding import PartitionSpec as P

P_SIZE = 512
NT = 16


def from_root(value, axis, source):
    kept = jnp.where(lax.axis_index(axis) == source, value, 0).astype(value.dtype)
    return lax.psum(kept, axis)


def reduce_by(left_side, right_side, free_dim):
    contract = 1 - free_dim
    return lax.dot_general(
        left_side,
        right_side,
        (((contract,), (contract,)), ((), ())),
        preferred_element_type=jnp.float32,
    )


def gather_corner(updated, panel_at, is_first):
    row_count = lax.axis_size("row")
    col_count = lax.axis_size("col")
    tile_rows = P_SIZE // row_count
    tile_cols = P_SIZE // col_count
    corner = updated[
        panel_at * tile_rows : (panel_at + 1) * tile_rows,
        panel_at * tile_cols : (panel_at + 1) * tile_cols,
    ]
    if is_first:
        pieces = lax.all_gather(
            corner.astype(jnp.bfloat16), ("row", "col"), axis=0, tiled=True
        ).astype(jnp.float32)
    else:
        pieces = lax.all_gather(corner, ("row", "col"), axis=0, tiled=True)
    return (
        pieces.reshape(row_count, col_count, tile_rows, tile_cols)
        .transpose(0, 2, 1, 3)
        .reshape(P_SIZE, P_SIZE)
    )


def transpose_rows(rounded, panel_at):
    row_count = lax.axis_size("row")
    col_count = lax.axis_size("col")
    group_size = row_count // col_count
    tile_rows = P_SIZE // row_count
    column_index = lax.axis_index("col")
    gathered = []
    for offset in range(group_size):
        gathered.append(from_root(rounded, "row", column_index * group_size + offset))
    stacked = jnp.stack(gathered)
    blocks = NT - 1 - panel_at
    reordered = stacked.reshape(group_size, blocks, tile_rows, P_SIZE).transpose(1, 0, 2, 3)
    return reordered.reshape(blocks * group_size * tile_rows, P_SIZE)


def solve_rows(updated, panel_at, is_first, corner_factor):
    tile_rows = P_SIZE // lax.axis_size("row")
    tile_cols = P_SIZE // lax.axis_size("col")
    below_rows = updated[
        (panel_at + 1) * tile_rows :, panel_at * tile_cols : (panel_at + 1) * tile_cols
    ]
    if is_first:
        panel_rows = lax.all_gather(
            below_rows.astype(jnp.bfloat16), "col", axis=1, tiled=True
        ).astype(jnp.float32)
    else:
        panel_rows = lax.all_gather(below_rows, "col", axis=1, tiled=True)
    solved = jax.scipy.linalg.solve_triangular(corner_factor, panel_rows.T, lower=True).T
    rounded = solved.astype(jnp.bfloat16)
    cross_part = transpose_rows(rounded, panel_at)
    own_tiles = lax.dynamic_slice_in_dim(solved, lax.axis_index("col") * tile_cols, tile_cols, 1)
    return (rounded, cross_part, own_tiles)


def panel_step(updated, panel_at, is_first):
    corner_block = gather_corner(updated, panel_at, is_first)
    corner_factor = jnp.linalg.cholesky(0.5 * (corner_block + corner_block.T))
    rounded, cross_part, own_tiles = solve_rows(updated, panel_at, is_first, corner_factor)
    free_dim = 0
    return (corner_factor, rounded, cross_part, own_tiles, free_dim)


def per_device(kernel):
    row_count = lax.axis_size("row")
    col_count = lax.axis_size("col")
    tile_rows = P_SIZE // row_count
    tile_cols = P_SIZE // col_count
    row_index = lax.axis_index("row")
    column_index = lax.axis_index("col")
    updated = kernel.reshape(NT, NT, tile_rows, tile_cols).transpose(0, 2, 1, 3)
    updated = updated.reshape(NT * tile_rows, NT * tile_cols).astype(jnp.float32)
    first_factor, first_rounded, first_cross, first_own, free_dim = panel_step(updated, 0, True)
    updated = updated.at[tile_rows:, tile_cols:].add(
        -reduce_by(first_rounded, first_cross, free_dim)
    )
    second_step = panel_step(updated, 1, False)
    second_factor, second_rounded, second_cross, second_own, free_dim = second_step
    updated = updated.at[2 * tile_rows :, 2 * tile_cols :].add(
        -reduce_by(second_rounded, second_cross, free_dim)
    )
    result = jnp.zeros_like(updated)
    result = result.at[2 * tile_rows :, 2 * tile_cols :].set(
        updated[2 * tile_rows :, 2 * tile_cols :]
    )
    start_row = row_index * tile_rows
    start_col = column_index * tile_cols
    first_corner = lax.dynamic_slice(first_factor, (start_row, start_col), (tile_rows, tile_cols))
    second_corner = lax.dynamic_slice(second_factor, (start_row, start_col), (tile_rows, tile_cols))
    result = result.at[:tile_rows, :tile_cols].set(first_corner)
    result = result.at[tile_rows:, :tile_cols].set(first_own)
    result = result.at[tile_rows : 2 * tile_rows, tile_cols : 2 * tile_cols].set(second_corner)
    result = result.at[2 * tile_rows :, tile_cols : 2 * tile_cols].set(second_own)
    tile_size = tile_rows * tile_cols
    result = result.reshape(NT, tile_rows, NT, tile_cols).transpose(0, 2, 1, 3)
    return result.reshape(NT, 1, NT, 1, tile_size)


def solution(mesh):
    placed = (P(None, "row", None, "col", None),)
    return jax.shard_map(
        per_device,
        mesh=mesh,
        in_specs=placed,
        out_specs=P(None, "row", None, "col", None),
        check_vma=False,
    )
```

profile of v0, /device:TPU:1, one launch (start us, length us, event | category | flops | bytes accessed | tf_op | source)
XLA Modules:
  0.0 938.9 jit_solution(17228424863130159677)
XLA Ops:
  9.7 30.5 %all_gather.13 = bf16[240,512]{0,1:T(8,128)(2,1)S(1)} all-gather(bf16[240,32]{0,1:T(8,128)(2,1)S(1)} %copy.26), channel_id=1, replica_groups=mesh['row'=32,'col'=16] {'col'}, dimensions={1}, use_global_device_ids=true | all-gather | bytes 261120 | tf_op jit(solution)/shard_map/all_gather | solution.py:69
  41.1 117.9 %all_gather.12 = bf16[8192,32]{1,0:T(8,128)(2,1)S(1)} all-gather(bf16[16,32]{1,0:T(8,128)(2,1)S(1)} %slice.328), channel_id=1, replica_groups=mesh['row'=32,'col'=16] {'row','col'}, dimensions={0}, use_global_device_ids=true | all-gather | bytes 525312 | tf_op jit(solution)/shard_map/all_gather | solution.py:35
  166.6 11.7 %cholesky.286 = f32[128,128]{1,0:T(8,128)S(1)} custom-call(f32[128,128]{1,0:T(8,128)S(1)} %cholesky.426), custom_call_target="Cholesky" | custom-call | tf_op jit(solution)/shard_map/jit(cholesky)/cholesky | solution.py:83
  178.4 9.8 %custom-call.33 = f32[1,128,128]{1,2,0:T(8,128)S(1)} custom-call(f32[1,128,128]{2,1,0:T(8,128)S(1)} %get-tuple-element.157), custom_call_target="InvertDiagBlocksLowerTriangular" | custom-call | tf_op jit(solution)/shard_map/jit(cholesky)/cholesky | solution.py:83
  189.0 11.7 %cholesky.305 = f32[128,128]{1,0:T(8,128)S(1)} custom-call(f32[128,128]{1,0:T(8,128)S(1)} %cholesky.430), custom_call_target="Cholesky" | custom-call | tf_op jit(solution)/shard_map/jit(cholesky)/cholesky | solution.py:83
  200.7 10.0 %custom-call.34 = f32[1,128,128]{1,2,0:T(8,128)S(1)} custom-call(f32[1,128,128]{2,1,0:T(8,128)S(1)} %get-tuple-element.154), custom_call_target="InvertDiagBlocksLowerTriangular" | custom-call | tf_op jit(solution)/shard_map/jit(cholesky)/cholesky | solution.py:83
  211.4 11.7 %cholesky.326 = f32[128,128]{1,0:T(8,128)S(1)} custom-call(f32[128,128]{1,0:T(8,128)S(1)} %cholesky.435), custom_call_target="Cholesky" | custom-call | tf_op jit(solution)/shard_map/jit(cholesky)/cholesky | solution.py:83
  223.8 9.8 %custom-call.35 = f32[1,128,128]{1,2,0:T(8,128)S(1)} custom-call(f32[1,128,128]{2,1,0:T(8,128)S(1)} %get-tuple-element.151), custom_call_target="InvertDiagBlocksLowerTriangular" | custom-call | tf_op jit(solution)/shard_map/jit(cholesky)/cholesky | solution.py:83
  234.2 11.9 %cholesky.343 = f32[128,128]{1,0:T(8,128)S(1)} custom-call(f32[128,128]{1,0:T(8,128)S(1)} %convolution_subtract_fusion.11), custom_call_target="Cholesky" | custom-call | tf_op jit(solution)/shard_map/jit(cholesky)/cholesky | solution.py:83
  250.3 8.1 while.9
  258.5 39.3 %custom-call.28 = f32[4,128,128]{1,2,0:T(8,128)S(1)} custom-call(f32[4,128,128]{2,1,0:T(8,128)S(1)} %get-tuple-element.97), custom_call_target="InvertDiagBlocksLowerTriangular" | custom-call | tf_op jit(solution)/shard_map/jit(_solve_triangular)/triangular_solve | solution.py:74
  303.6 133.9 %all-reduce.9.cloned.1.call-done = (bf16[1,15,16,512]{3,2,0,1:T(8,128)(2,1)}, bf16[1,15,16,512]{3,2,0,1:T(8,128)(2,1)}) async-done(((bf16[1,15,16,512]{3,2,0,1:T(8,128)(2,1)}, bf16[1,15,16,512]{3,2,0,1:T(8,128)(2,1)}), (bf16[1,15,16,512]{3,2,0,1:T(8,128)(2,1)}, bf16[1,15,16,512]{3,2,0,1:T(8,128)(2,1)})) %all-reduce.9.cloned.1.call-update) | async-done | bytes 491536 | tf_op jit(solution)/shard_map/psum | solution.py:12
  440.9 27.0 %all_gather.15 = f32[224,512]{0,1:T(8,128)S(1)} all-gather(f32[224,32]{0,1:T(8,128)S(1)} %copy.33), channel_id=1, replica_groups=mesh['row'=32,'col'=16] {'col'}, dimensions={1}, use_global_device_ids=true | all-gather | bytes 487424 | tf_op jit(solution)/shard_map/all_gather | solution.py:73
  468.9 171.9 %all-gather.2.cloned.1.call-done = f32[8192,32]{1,0:T(8,128)} async-done(((f32[16,32]{1,0:T(8,128)}), f32[8192,32]{1,0:T(8,128)}) %all-gather.2.cloned.1.call-update) | async-done | bytes 1048592 | tf_op jit(solution)/shard_map/all_gather | solution.py:39
  651.8 11.7 %cholesky.358 = f32[128,128]{1,0:T(8,128)S(1)} custom-call(f32[128,128]{1,0:T(8,128)S(1)} %cholesky.439), custom_call_target="Cholesky" | custom-call | tf_op jit(solution)/shard_map/jit(cholesky)/cholesky | solution.py:83
  664.3 9.8 %custom-call.36 = f32[1,128,128]{1,2,0:T(8,128)S(1)} custom-call(f32[1,128,128]{2,1,0:T(8,128)S(1)} %get-tuple-element.147), custom_call_target="InvertDiagBlocksLowerTriangular" | custom-call | tf_op jit(solution)/shard_map/jit(cholesky)/cholesky | solution.py:83
  674.9 11.7 %cholesky.377 = f32[128,128]{1,0:T(8,128)S(1)} custom-call(f32[128,128]{1,0:T(8,128)S(1)} %cholesky.443), custom_call_target="Cholesky" | custom-call | tf_op jit(solution)/shard_map/jit(cholesky)/cholesky | solution.py:83
  687.3 9.9 %custom-call.37 = f32[1,128,128]{1,2,0:T(8,128)S(1)} custom-call(f32[1,128,128]{2,1,0:T(8,128)S(1)} %get-tuple-element.144), custom_call_target="InvertDiagBlocksLowerTriangular" | custom-call | tf_op jit(solution)/shard_map/jit(cholesky)/cholesky | solution.py:83
  697.9 11.7 %cholesky.398 = f32[128,128]{1,0:T(8,128)S(1)} custom-call(f32[128,128]{1,0:T(8,128)S(1)} %cholesky.448), custom_call_target="Cholesky" | custom-call | tf_op jit(solution)/shard_map/jit(cholesky)/cholesky | solution.py:83
  710.3 9.8 %custom-call.38 = f32[1,128,128]{1,2,0:T(8,128)S(1)} custom-call(f32[1,128,128]{2,1,0:T(8,128)S(1)} %get-tuple-element.141), custom_call_target="InvertDiagBlocksLowerTriangular" | custom-call | tf_op jit(solution)/shard_map/jit(cholesky)/cholesky | solution.py:83
  720.7 11.9 %cholesky.415 = f32[128,128]{1,0:T(8,128)S(1)} custom-call(f32[128,128]{1,0:T(8,128)S(1)} %convolution_subtract_fusion.10), custom_call_target="Cholesky" | custom-call | tf_op jit(solution)/shard_map/jit(cholesky)/cholesky | solution.py:83
  736.3 8.1 while.10
  744.5 39.3 %custom-call.29 = f32[4,128,128]{1,2,0:T(8,128)S(1)} custom-call(f32[4,128,128]{2,1,0:T(8,128)S(1)} %get-tuple-element.105), custom_call_target="InvertDiagBlocksLowerTriangular" | custom-call | tf_op jit(solution)/shard_map/jit(_solve_triangular)/triangular_solve | solution.py:74
  790.5 128.8 %all-reduce.7.cloned.1.call-done = (bf16[1,14,16,512]{3,2,0,1:T(8,128)(2,1)}, bf16[1,14,16,512]{3,2,0,1:T(8,128)(2,1)}) async-done(((bf16[1,14,16,512]{3,2,0,1:T(8,128)(2,1)}, bf16[1,14,16,512]{3,2,0,1:T(8,128)(2,1)}), (bf16[1,14,16,512]{3,2,0,1:T(8,128)(2,1)}, bf16[1,14,16,512]{3,2,0,1:T(8,128)(2,1)})) %all-reduce.7.cloned.1.call-update) | async-done | bytes 458768 | tf_op jit(solution)/shard_map/psum | solution.py:12
  (135 shorter events, 77.9 us)
Async XLA Ops:
  6.5 430.9 %all-reduce.9.cloned.1.call-start = ((), (), s32[]{:S(2)}) async-start(), calls=%async_computation.2 | async-start | bytes 983040 | tf_op jit(solution)/shard_map/psum | solution.py:12
  9.5 151.9 %copy-start.2 = (bf16[256,512]{1,0:T(8,128)(2,1)}, bf16[256,512]{1,0:T(8,128)(2,1)S(1)}, u32[]{:S(2)}) copy-start(bf16[256,512]{1,0:T(8,128)(2,1)S(1)} %convert_element_type.30) | copy-start | bytes 786436
  303.5 337.3 %all-gather.2.cloned.1.call-start = ((), (), s32[]{:S(2)}) async-start(), calls=%async_computation | async-start | bytes 4202496 | tf_op jit(solution)/shard_map/all_gather | solution.py:39
  439.8 1.0 copy-start
  440.5 478.8 %all-reduce.7.cloned.1.call-start = ((), (), s32[]{:S(2)}) async-start(), calls=%async_computation.1 | async-start | bytes 917504 | tf_op jit(solution)/shard_map/psum | solution.py:12
  736.2 184.2 %copy-start.1 = (f32[240,480]{1,0:T(8,128)S(1)}, f32[240,480]{1,0:T(8,128)}, u32[]{:S(2)}) copy-start(f32[240,480]{1,0:T(8,128)} %copy-done) | copy-start | bytes 1382404
Sparse Core Ops, SparseCore 0:
  303.6 133.7 all-reduce.8
  442.9 197.9 all-gather.1
  790.5 128.7 all-reduce.6
where the time goes:
time: 944 us; the launch traced here: 939 us
  waiting for transfers between devices  435 us (46%)
  other arithmetic  243 us (26%)
  blocking collectives  175 us (19%)
  local copies, waits for them, and re-layouts  50.7 us (5%)
  between operations  19 us (2%)
  matrix products  15.8 us (2%)
    psum x2, waiting for transfers between devices, from_root(): return lax.psum(kept, axis)  263 us
    all_gather x1, waiting for transfers between devices, gather_corner(): pieces = lax.all_gather(corner, ('row', 'col'), axis=0, tiled=True)  172 us
    another operation x29, other arithmetic, panel_step(): corner_factor = jnp.linalg.cholesky(0.5 * (corner_block + corner_block.T))  158 us
    all_gather x1, blocking collectives, gather_corner(): lax.all_gather(corner.astype(jnp.bfloat16), ('row', 'col'), axis=0, tiled...  118 us
    another operation x7, other arithmetic, solve_rows(): jax.scipy.linalg.solve_triangular(corner_factor, panel_rows.T, lower=True)  79.2 us
    all_gather x1, blocking collectives, solve_rows(): lax.all_gather(below_rows.astype(jnp.bfloat16), 'col', axis=1, tiled=True)  30.5 us
    all_gather x1, blocking collectives, solve_rows(): panel_rows = lax.all_gather(below_rows, 'col', axis=1, tiled=True)  27 us
  transfers between devices with their start and end apart: 3, of which 3 were waited for; matrix products, arithmetic and copies ran while one was open for 0% of the time, Pallas kernels for 0%

commit v1 on v0

v1 whole, which is shorter than its diff:
```python
import jax
import jax.numpy as jnp
from jax import lax
from jax.sharding import PartitionSpec as P

P_SIZE = 512
NT = 16


def bf16_gram(left_side, right_side):
    return lax.dot_general(
        left_side.astype(jnp.bfloat16),
        right_side.astype(jnp.bfloat16),
        (((1,), (1,)), ((), ())),
        preferred_element_type=jnp.float32,
    )


def right_solve(factor, rows):
    return jax.scipy.linalg.solve_triangular(factor, rows.T, lower=True).T


def lower_factor(block):
    return jnp.linalg.cholesky(0.5 * (block + block.T))


def per_device(kernel):
    row_count = lax.axis_size("row")
    col_count = lax.axis_size("col")
    tile_rows = P_SIZE // row_count
    tile_cols = P_SIZE // col_count
    row_index = lax.axis_index("row")
    column_index = lax.axis_index("col")
    tiles = kernel.reshape(NT, NT, tile_rows, tile_cols)
    local = tiles.transpose(0, 2, 1, 3).reshape(NT * tile_rows, NT * tile_cols)

    with jax.named_scope("gather_inputs"):
        corner_tiles = jnp.stack([tiles[0, 0], tiles[1, 0], tiles[1, 1]])
        corners = lax.all_gather(corner_tiles, ("row", "col"), axis=0)
        corners = corners.reshape(row_count, col_count, 3, tile_rows, tile_cols)
        corners = corners.transpose(2, 0, 3, 1, 4).reshape(3, P_SIZE, P_SIZE)
        corners = corners.astype(jnp.float32)
        own_rows = lax.all_gather(local[tile_rows:, : 2 * tile_cols], "col", axis=0)
        own_rows = own_rows.reshape(col_count, (NT - 1) * tile_rows, 2, tile_cols)
        own_rows = own_rows.transpose(1, 2, 0, 3).reshape((NT - 1) * tile_rows, 2 * P_SIZE)
        own_rows = own_rows.astype(jnp.float32)
        col_rows = lax.all_gather(local[: 2 * tile_rows, tile_cols:], "row", axis=0)
        col_rows = col_rows.reshape(row_count, 2, tile_rows, (NT - 1) * tile_cols)
        col_rows = col_rows.transpose(3, 1, 0, 2).reshape((NT - 1) * tile_cols, 2 * P_SIZE)
        col_rows = col_rows.astype(jnp.float32)

    with jax.named_scope("first_panel"):
        first_factor = lower_factor(corners[0])
        own_count = (NT - 1) * tile_rows
        col_total = (NT - 1) * tile_cols
        stacked = jnp.concatenate(
            [corners[1], own_rows[:, :P_SIZE], col_rows[:, :P_SIZE]], axis=0
        )
        solved = right_solve(first_factor, stacked)
        next_rows = solved[:P_SIZE].astype(jnp.bfloat16)
        first_own = solved[P_SIZE : P_SIZE + own_count]
        first_col = solved[P_SIZE + own_count :]

    with jax.named_scope("second_panel"):
        second_corner = corners[2] - bf16_gram(next_rows, next_rows)
        second_factor = lower_factor(second_corner)
        own_below = own_rows[tile_rows:, P_SIZE:] - bf16_gram(first_own[tile_rows:], next_rows)
        col_below = col_rows[tile_cols:, P_SIZE:] - bf16_gram(first_col[tile_cols:], next_rows)
        solved = right_solve(second_factor, jnp.concatenate([own_below, col_below], axis=0))
        second_own = solved[: own_count - tile_rows]
        second_col = solved[own_count - tile_rows :]

    with jax.named_scope("trailing_update"):
        trailing = local[2 * tile_rows :, 2 * tile_cols :]
        trailing = trailing.astype(jnp.float32) - bf16_gram(
            first_own[tile_rows:], first_col[tile_cols:]
        )
        trailing = trailing - bf16_gram(second_own, second_col)

    with jax.named_scope("assemble"):
        start_row = row_index * tile_rows
        start_col = column_index * tile_cols
        first_corner = lax.dynamic_slice(first_factor, (start_row, start_col), (tile_rows, tile_cols))
        second_tile = lax.dynamic_slice(second_factor, (start_row, start_col), (tile_rows, tile_cols))
        first_cols = lax.dynamic_slice_in_dim(first_own, start_col, tile_cols, 1)
        second_cols = lax.dynamic_slice_in_dim(second_own, start_col, tile_cols, 1)
        result = jnp.zeros((NT * tile_rows, NT * tile_cols), jnp.float32)
        result = result.at[:tile_rows, :tile_cols].set(first_corner)
        result = result.at[tile_rows:, :tile_cols].set(first_cols)
        result = result.at[tile_rows : 2 * tile_rows, tile_cols : 2 * tile_cols].set(second_tile)
        result = result.at[2 * tile_rows :, tile_cols : 2 * tile_cols].set(second_cols)
        result = result.at[2 * tile_rows :, 2 * tile_cols :].set(trailing)
        result = result.reshape(NT, tile_rows, NT, tile_cols).transpose(0, 2, 1, 3)
    return result.reshape(NT, 1, NT, 1, tile_rows * tile_cols)


def solution(mesh):
    placed = (P(None, "row", None, "col", None),)
    return jax.shard_map(
        per_device,
        mesh=mesh,
        in_specs=placed,
        out_specs=P(None, "row", None, "col", None),
        check_vma=False,
    )
```

time: 944 us -> 578 us (0.61)
  waiting for transfers between devices: 435 us -> 144 us
  blocking collectives: 175 us -> 58.1 us
  local copies, waits for them, and re-layouts: 50.7 us -> 76 us
  other arithmetic: 243 us -> 254 us
    psum x2 -> x0, waiting for transfers between devices: 263 us -> none  [from_root(): return lax.psum(kept, axis)]
    all_gather x3 -> x2, blocking collectives: 175 us -> 58.1 us  [the longest x1 29.5 us: per_device(): own_rows = lax.all_gather(local[tile_rows:, :2 * tile_cols], 'col', axis=0)]
    all_gather x1, waiting for transfers between devices: 172 us -> 144 us  [per_device(): corners = lax.all_gather(corner_tiles, ('row', 'col'), axis=0)]
    slice x6 -> x12, local copies, waits for them, and re-layouts: 0.8 us -> 23.9 us  [the longest x2 13.1 us: per_device(): second_corner = corners[2] - bf16_gram(next_rows, next_rows)]
    reshape x7 -> x3, local copies, waits for them, and re-layouts: 20 us -> 5.84 us  [the longest x1 3.13 us: per_device(): return result.reshape(NT, 1, NT, 1, tile_rows * tile_cols)]
    squeeze x0 -> x5, local copies, waits for them, and re-layouts: none -> 11.6 us  [the longest x2 4.05 us: per_device(): first_factor = lower_factor(corners[0])]
    another operation x38 -> x36, other arithmetic: 240 us -> 241 us  [the longest x29 158 us: lower_factor(): return jnp.linalg.cholesky(0.5 * (block + block.T))]
  transfers between devices with their start and end apart: 3 -> 1, of which waited for: 3 -> 1; matrix products, arithmetic and copies ran while one was open for 0% -> 1% of each run, Pallas kernels for 0% -> 0%
where the time goes in v1:
time: 578 us; the launch traced here: 570 us
  other arithmetic  254 us (44%)
  waiting for transfers between devices  144 us (25%)
  local copies, waits for them, and re-layouts  76 us (13%)
  blocking collectives  58.1 us (10%)
  between operations  19.3 us (3%)
  matrix products  18.4 us (3%)
    another operation x29, other arithmetic, lower_factor(): return jnp.linalg.cholesky(0.5 * (block + block.T))  158 us
    all_gather x1, waiting for transfers between devices, per_device(): corners = lax.all_gather(corner_tiles, ('row', 'col'), axis=0)  144 us
    another operation x5, other arithmetic, right_solve(): return jax.scipy.linalg.solve_triangular(factor, rows.T, lower=True).T  81.7 us
    all_gather x1, blocking collectives, per_device(): own_rows = lax.all_gather(local[tile_rows:, :2 * tile_cols], 'col', axis=0)  29.5 us
    all_gather x1, blocking collectives, per_device(): col_rows = lax.all_gather(local[:2 * tile_rows, tile_cols:], 'row', axis=0)  28.7 us
    another operation x24, local copies, waits for them, and re-layouts  16.1 us
    slice x2, local copies, waits for them, and re-layouts, per_device(): second_corner = corners[2] - bf16_gram(next_rows, next_rows)  13.1 us
  transfers between devices with their start and end apart: 1, of which 1 were waited for; matrix products, arithmetic and copies ran while one was open for 1% of the time, Pallas kernels for 0%

profile of v1, /device:TPU:1, one launch (start us, length us, event | category | flops | bytes accessed | tf_op | source)
XLA Modules:
  0.0 570.0 jit_solution(10384111964324473233)
XLA Ops:
  10.3 28.7 %all-gather.2 = bf16[1024,480]{1,0:T(8,128)(2,1)S(1)} all-gather(bf16[32,480]{1,0:T(8,128)(2,1)S(1)} %slice.351), channel_id=4, replica_groups=mesh['row'=32,'col'=16] {'row'}, dimensions={0}, use_global_device_ids=true | all-gather | bytes 1013760 | tf_op jit(solution)/shard_map/gather_inputs/all_gather | solution.py:47
  39.7 29.5 %all-gather.3 = bf16[16,240,64]{1,2,0:T(8,128)(2,1)S(1)} all-gather(bf16[1,240,64]{1,2,0:T(8,128)(2,1)S(1)} %copy.46), channel_id=3, replica_groups=mesh['row'=32,'col'=16] {'col'}, dimensions={0}, use_global_device_ids=true | all-gather | bytes 522240 | tf_op jit(solution)/shard_map/gather_inputs/all_gather | solution.py:43
  74.2 143.7 %all-gather.6.cloned.1.call-done = bf16[1536,16,32]{2,1,0:T(8,128)(2,1)} async-done(((bf16[3,16,32]{2,1,0:T(8,128)(2,1)}), bf16[1536,16,32]{2,1,0:T(8,128)(2,1)}) %all-gather.6.cloned.1.call-update) | async-done | bytes 1572880 | tf_op jit(solution)/shard_map/gather_inputs/all_gather | solution.py:39
  217.9 9.0 %convert_bitcast_fusion = f32[3,32,16,16,32]{4,2,0,3,1:T(8,128)} fusion(bf16[32,16,3,16,32]{4,3,2,1,0:T(8,128)(2,1)} %bitcast.155), kind=kLoop, calls=%fused_computation.4 | loop fusion | flops 786432 | bytes 4718592 | tf_op jit(solution)/shard_map/gather_inputs/convert_element_type | solution.py:42
  226.9 9.4 %fusion.76 = (f32[1,32,16,16,32]{4,2,0,3,1:T(8,128)}, f32[1,32,16,16,32]{4,2,0,3,1:T(8,128)}, f32[1,32,16,16,32]{4,2,0,3,1:T(8,128)S(1)}) fusion(f32[3,32,16,16,32]{4,2,0,3,1:T(8,128)} %convert_bitcast_fusion), kind=kLoop, calls=%fused_computation.163 | loop fusion | bytes 6291456 | tf_op jit(solution)/shard_map/second_panel/slice | solution.py:65
  244.9 11.7 %cholesky.286 = f32[128,128]{1,0:T(8,128)S(1)} custom-call(f32[128,128]{1,0:T(8,128)S(1)} %cholesky.426), custom_call_target="Cholesky" | custom-call | tf_op jit(solution)/shard_map/first_panel/jit(cholesky)/cholesky | solution.py:24
  256.6 9.8 %custom-call.33 = f32[1,128,128]{1,2,0:T(8,128)S(1)} custom-call(f32[1,128,128]{2,1,0:T(8,128)S(1)} %get-tuple-element.131), custom_call_target="InvertDiagBlocksLowerTriangular" | custom-call | tf_op jit(solution)/shard_map/first_panel/jit(cholesky)/cholesky | solution.py:24
  267.2 11.7 %cholesky.305 = f32[128,128]{1,0:T(8,128)S(1)} custom-call(f32[128,128]{1,0:T(8,128)S(1)} %cholesky.430), custom_call_target="Cholesky" | custom-call | tf_op jit(solution)/shard_map/first_panel/jit(cholesky)/cholesky | solution.py:24
  279.0 10.2 %custom-call.34 = f32[1,128,128]{1,2,0:T(8,128)S(1)} custom-call(f32[1,128,128]{2,1,0:T(8,128)S(1)} %get-tuple-element.128), custom_call_target="InvertDiagBlocksLowerTriangular" | custom-call | tf_op jit(solution)/shard_map/first_panel/jit(cholesky)/cholesky | solution.py:24
  289.8 11.7 %cholesky.326 = f32[128,128]{1,0:T(8,128)S(1)} custom-call(f32[128,128]{1,0:T(8,128)S(1)} %cholesky.435), custom_call_target="Cholesky" | custom-call | tf_op jit(solution)/shard_map/first_panel/jit(cholesky)/cholesky | solution.py:24
  302.3 9.8 %custom-call.35 = f32[1,128,128]{1,2,0:T(8,128)S(1)} custom-call(f32[1,128,128]{2,1,0:T(8,128)S(1)} %get-tuple-element.125), custom_call_target="InvertDiagBlocksLowerTriangular" | custom-call | tf_op jit(solution)/shard_map/first_panel/jit(cholesky)/cholesky | solution.py:24
  312.7 11.9 %cholesky.343 = f32[128,128]{1,0:T(8,128)S(1)} custom-call(f32[128,128]{1,0:T(8,128)S(1)} %convolution_subtract_fusion.16), custom_call_target="Cholesky" | custom-call | tf_op jit(solution)/shard_map/first_panel/jit(cholesky)/cholesky | solution.py:24
  329.7 8.1 %while.7 = (s32[]{:T(128)}, f32[512,512]{1,0:T(8,128)S(1)}, s32[4,2]{0,1:T(2,128)S(1)}, f32[4,128,128]{2,1,0:T(8,128)S(1)}, s32[]{:T(128)}) while((s32[]{:T(128)}, f32[512,512]{1,0:T(8,128)S(1)}, s32[4,2]{0,1:T(2,128)S(1)}, f32[4,128,128]{2,1,0:T(8,128)S(1)}, s32[]{:T(128)}) %tuple.75), condition=%wide.while_cond.5, body=%wide.while_body.5.sunk | while | flops 2 | bytes 131181 | solution.py:20
  337.9 39.9 %custom-call.28 = f32[4,128,128]{1,2,0:T(8,128)} custom-call(f32[4,128,128]{2,1,0:T(8,128)S(1)} %get-tuple-element.73), custom_call_target="InvertDiagBlocksLowerTriangular" | custom-call | tf_op jit(solution)/shard_map/first_panel/jit(_solve_triangular)/triangular_solve | solution.py:20
  377.8 5.8 %copy.44 = f32[1,32,16,16,32]{4,3,2,1,0:T(8,128)} copy(f32[1,32,16,16,32]{4,2,0,3,1:T(8,128)} %get-tuple-element.107) | data formatting | bytes 2097152 | tf_op jit(solution)/shard_map/first_panel/slice | solution.py:57
  409.8 11.7 %cholesky.358 = f32[128,128]{1,0:T(8,128)S(1)} custom-call(f32[128,128]{1,0:T(8,128)S(1)} %cholesky.439), custom_call_target="Cholesky" | custom-call | tf_op jit(solution)/shard_map/second_panel/jit(cholesky)/cholesky | solution.py:24
  421.7 9.8 %custom-call.36 = f32[1,128,128]{1,2,0:T(8,128)S(1)} custom-call(f32[1,128,128]{2,1,0:T(8,128)S(1)} %get-tuple-element.121), custom_call_target="InvertDiagBlocksLowerTriangular" | custom-call | tf_op jit(solution)/shard_map/second_panel/jit(cholesky)/cholesky | solution.py:24
  432.2 11.7 %cholesky.377 = f32[128,128]{1,0:T(8,128)S(1)} custom-call(f32[128,128]{1,0:T(8,128)S(1)} %cholesky.443), custom_call_target="Cholesky" | custom-call | tf_op jit(solution)/shard_map/second_panel/jit(cholesky)/cholesky | solution.py:24
  445.3 10.0 %custom-call.37 = f32[1,128,128]{1,2,0:T(8,128)S(1)} custom-call(f32[1,128,128]{2,1,0:T(8,128)S(1)} %get-tuple-element.118), custom_call_target="InvertDiagBlocksLowerTriangular" | custom-call | tf_op jit(solution)/shard_map/second_panel/jit(cholesky)/cholesky | solution.py:24
  455.9 11.7 %cholesky.398 = f32[128,128]{1,0:T(8,128)S(1)} custom-call(f32[128,128]{1,0:T(8,128)S(1)} %cholesky.448), custom_call_target="Cholesky" | custom-call | tf_op jit(solution)/shard_map/second_panel/jit(cholesky)/cholesky | solution.py:24
  468.3 9.8 %custom-call.38 = f32[1,128,128]{1,2,0:T(8,128)S(1)} custom-call(f32[1,128,128]{2,1,0:T(8,128)S(1)} %get-tuple-element.115), custom_call_target="InvertDiagBlocksLowerTriangular" | custom-call | tf_op jit(solution)/shard_map/second_panel/jit(cholesky)/cholesky | solution.py:24
  478.7 11.9 %cholesky.415 = f32[128,128]{1,0:T(8,128)S(1)} custom-call(f32[128,128]{1,0:T(8,128)S(1)} %convolution_subtract_fusion.15), custom_call_target="Cholesky" | custom-call | tf_op jit(solution)/shard_map/second_panel/jit(cholesky)/cholesky | solution.py:24
  495.2 8.1 %while.8 = (s32[]{:T(128)}, f32[512,512]{1,0:T(8,128)S(1)}, s32[4,2]{0,1:T(2,128)S(1)}, f32[4,128,128]{2,1,0:T(8,128)S(1)}, s32[]{:T(128)}) while((s32[]{:T(128)}, f32[512,512]{1,0:T(8,128)S(1)}, s32[4,2]{0,1:T(2,128)S(1)}, f32[4,128,128]{2,1,0:T(8,128)S(1)}, s32[]{:T(128)}) %tuple.83), condition=%wide.while_cond.6, body=%wide.while_body.6.sunk | while | flops 2 | bytes 131181 | solution.py:20
  503.4 39.3 %custom-call.29 = f32[4,128,128]{1,2,0:T(8,128)S(1)} custom-call(f32[4,128,128]{2,1,0:T(8,128)S(1)} %get-tuple-element.81), custom_call_target="InvertDiagBlocksLowerTriangular" | custom-call | tf_op jit(solution)/shard_map/second_panel/jit(_solve_triangular)/triangular_solve | solution.py:20
  (154 shorter events, 91.7 us)
Async XLA Ops:
  6.5 211.4 %all-gather.6.cloned.1.call-start = ((), (), s32[]{:S(2)}) async-start(), calls=%async_computation | async-start | bytes 6303744 | tf_op jit(solution)/shard_map/gather_inputs/all_gather | solution.py:39
  383.6 3.6 copy-start.1
  387.3 1.3 copy-start.7
  396.8 1.2 copy-start.2
  396.8 2.6 copy-start.4
  398.0 2.6 copy-start
  493.9 48.8 %copy-start.3 = (f32[448,512]{1,0:T(8,128)S(1)}, f32[448,512]{1,0:T(8,128)}, u32[]{:S(2)}) copy-start(f32[448,512]{1,0:T(8,128)} %convolution_subtract_fusion.4) | copy-start | bytes 2752516
  493.9 48.8 %copy-start.5 = (f32[224,512]{1,0:T(8,128)S(1)}, f32[224,512]{1,0:T(8,128)}, u32[]{:S(2)}) copy-start(f32[224,512]{1,0:T(8,128)} %convolution_subtract_fusion.7) | copy-start | bytes 1376260
  546.8 1.0 copy-start.6
  547.8 1.0 slice-start
Sparse Core Ops, SparseCore 0:
  11.8 206.1 all-gather.5

commit v2 on v1

--- a/solution.py
+++ b/solution.py
@@ -36,7 +36,7 @@
 
     with jax.named_scope("gather_inputs"):
         corner_tiles = jnp.stack([tiles[0, 0], tiles[1, 0], tiles[1, 1]])
-        corners = lax.all_gather(corner_tiles, ("row", "col"), axis=0)
+        corners = lax.all_gather(corner_tiles.reshape(1, -1), ("row", "col"), axis=0, tiled=True)
         corners = corners.reshape(row_count, col_count, 3, tile_rows, tile_cols)
         corners = corners.transpose(2, 0, 3, 1, 4).reshape(3, P_SIZE, P_SIZE)
         corners = corners.astype(jnp.float32)

time: 578 us -> 577 us (level)
  local copies, waits for them, and re-layouts: 76 us -> 82.7 us
  waiting for transfers between devices: 144 us -> 138 us
    convert_element_type x0 -> x1, local copies, waits for them, and re-layouts: none -> 6.21 us  [per_device(): corners = corners.astype(jnp.float32)]
    all_gather x1, waiting for transfers between devices: 144 us -> 138 us  [per_device(): lax.all_gather(corner_tiles.reshape(1, -1), ('row', 'col'), axis=0, tiled...]
where the time goes in v2:
time: 577 us; the launch traced here: 573 us
  other arithmetic  256 us (44%)
  waiting for transfers between devices  138 us (24%)
  local copies, waits for them, and re-layouts  82.7 us (14%)
  blocking collectives  58.6 us (10%)
  between operations  19.4 us (3%)
  matrix products  18.4 us (3%)
    another operation x29, other arithmetic, lower_factor(): return jnp.linalg.cholesky(0.5 * (block + block.T))  158 us
    all_gather x1, waiting for transfers between devices, per_device(): lax.all_gather(corner_tiles.reshape(1, -1), ('row', 'col'), axis=0, tiled...  138 us
    another operation x5, other arithmetic, right_solve(): return jax.scipy.linalg.solve_triangular(factor, rows.T, lower=True).T  81.7 us
    all_gather x1, blocking collectives, per_device(): own_rows = lax.all_gather(local[tile_rows:, :2 * tile_cols], 'col', axis=0)  29.9 us
    all_gather x1, blocking collectives, per_device(): col_rows = lax.all_gather(local[:2 * tile_rows, tile_cols:], 'row', axis=0)  28.7 us
    another operation x24, local copies, waits for them, and re-layouts  16.1 us
    slice x2, local copies, waits for them, and re-layouts, per_device(): second_corner = corners[2] - bf16_gram(next_rows, next_rows)  13.1 us
  transfers between devices with their start and end apart: 1, of which 1 were waited for; matrix products, arithmetic and copies ran while one was open for 1% of the time, Pallas kernels for 0%

profile of v2, /device:TPU:1, one launch (start us, length us, event | category | flops | bytes accessed | tf_op | source)
XLA Modules:
  0.0 572.8 jit_solution(107486555777567554)
XLA Ops:
  10.4 28.7 %all-gather.1 = bf16[1024,480]{1,0:T(8,128)(2,1)S(1)} all-gather(bf16[32,480]{1,0:T(8,128)(2,1)S(1)} %slice.351), channel_id=3, replica_groups=mesh['row'=32,'col'=16] {'row'}, dimensions={0}, use_global_device_ids=true | all-gather | bytes 1013760 | tf_op jit(solution)/shard_map/gather_inputs/all_gather | solution.py:47
  39.8 29.9 %all-gather.3 = bf16[16,240,64]{1,2,0:T(8,128)(2,1)S(1)} all-gather(bf16[1,240,64]{1,2,0:T(8,128)(2,1)S(1)} %copy.46), channel_id=2, replica_groups=mesh['row'=32,'col'=16] {'col'}, dimensions={0}, use_global_device_ids=true | all-gather | bytes 522240 | tf_op jit(solution)/shard_map/gather_inputs/all_gather | solution.py:43
  74.8 137.8 %all-gather.6.cloned.1.call-done = bf16[512,1,1536]{2,1,0:T(2,128)(2,1)} async-done(((bf16[1,1,1536]{2,1,0:T(2,128)(2,1)}), bf16[512,1,1536]{2,1,0:T(2,128)(2,1)}) %all-gather.6.cloned.1.call-update) | async-done | bytes 1572880 | tf_op jit(solution)/shard_map/gather_inputs/all_gather | solution.py:39
  212.6 11.1 %convert_reduce_fusion = f32[512,1536]{1,0:T(8,128)S(1)} fusion(bf16[512,1,1536]{2,1,0:T(2,128)(2,1)} %all-gather.6.cloned.1.call-done), kind=kLoop, calls=%fused_computation.4 | loop fusion | flops 786432 | bytes 4718592 | tf_op jit(solution)/shard_map/gather_inputs/convert_element_type | solution.py:42
  223.7 6.2 %reshape.279 = f32[32,16,3,16,32]{4,3,2,1,0:T(8,128)} reshape(f32[512,1536]{1,0:T(8,128)S(1)} %convert_reduce_fusion) | data formatting | bytes 6291456 | tf_op jit(solution)/shard_map/gather_inputs/convert_element_type | solution.py:42
  229.9 9.4 %fusion.76 = (f32[1,32,16,16,32]{4,2,0,3,1:T(8,128)}, f32[1,32,16,16,32]{4,2,0,3,1:T(8,128)}, f32[1,32,16,16,32]{4,2,0,3,1:T(8,128)S(1)}) fusion(f32[3,32,16,16,32]{4,2,0,3,1:T(8,128)} %bitcast.151), kind=kLoop, calls=%fused_computation.164 | loop fusion | bytes 6291456 | tf_op jit(solution)/shard_map/second_panel/slice | solution.py:65
  247.7 11.7 %cholesky.286 = f32[128,128]{1,0:T(8,128)S(1)} custom-call(f32[128,128]{1,0:T(8,128)S(1)} %cholesky.426), custom_call_target="Cholesky" | custom-call | tf_op jit(solution)/shard_map/first_panel/jit(cholesky)/cholesky | solution.py:24
  259.5 9.8 %custom-call.33 = f32[1,128,128]{1,2,0:T(8,128)S(1)} custom-call(f32[1,128,128]{2,1,0:T(8,128)S(1)} %get-tuple-element.131), custom_call_target="InvertDiagBlocksLowerTriangular" | custom-call | tf_op jit(solution)/shard_map/first_panel/jit(cholesky)/cholesky | solution.py:24
  270.1 11.7 %cholesky.305 = f32[128,128]{1,0:T(8,128)S(1)} custom-call(f32[128,128]{1,0:T(8,128)S(1)} %cholesky.430), custom_call_target="Cholesky" | custom-call | tf_op jit(solution)/shard_map/first_panel/jit(cholesky)/cholesky | solution.py:24
  281.8 10.2 %custom-call.34 = f32[1,128,128]{1,2,0:T(8,128)S(1)} custom-call(f32[1,128,128]{2,1,0:T(8,128)S(1)} %get-tuple-element.128), custom_call_target="InvertDiagBlocksLowerTriangular" | custom-call | tf_op jit(solution)/shard_map/first_panel/jit(cholesky)/cholesky | solution.py:24
  292.7 11.7 %cholesky.326 = f32[128,128]{1,0:T(8,128)S(1)} custom-call(f32[128,128]{1,0:T(8,128)S(1)} %cholesky.435), custom_call_target="Cholesky" | custom-call | tf_op jit(solution)/shard_map/first_panel/jit(cholesky)/cholesky | solution.py:24
  305.1 9.8 %custom-call.35 = f32[1,128,128]{1,2,0:T(8,128)S(1)} custom-call(f32[1,128,128]{2,1,0:T(8,128)S(1)} %get-tuple-element.125), custom_call_target="InvertDiagBlocksLowerTriangular" | custom-call | tf_op jit(solution)/shard_map/first_panel/jit(cholesky)/cholesky | solution.py:24
  315.6 11.9 %cholesky.343 = f32[128,128]{1,0:T(8,128)S(1)} custom-call(f32[128,128]{1,0:T(8,128)S(1)} %convolution_subtract_fusion.16), custom_call_target="Cholesky" | custom-call | tf_op jit(solution)/shard_map/first_panel/jit(cholesky)/cholesky | solution.py:24
  332.6 8.1 %while.7 = (s32[]{:T(128)}, f32[512,512]{1,0:T(8,128)S(1)}, s32[4,2]{0,1:T(2,128)S(1)}, f32[4,128,128]{2,1,0:T(8,128)S(1)}, s32[]{:T(128)}) while((s32[]{:T(128)}, f32[512,512]{1,0:T(8,128)S(1)}, s32[4,2]{0,1:T(2,128)S(1)}, f32[4,128,128]{2,1,0:T(8,128)S(1)}, s32[]{:T(128)}) %tuple.75), condition=%wide.while_cond.5, body=%wide.while_body.5.sunk | while | flops 2 | bytes 131181 | solution.py:20
  340.7 39.9 %custom-call.28 = f32[4,128,128]{1,2,0:T(8,128)} custom-call(f32[4,128,128]{2,1,0:T(8,128)S(1)} %get-tuple-element.73), custom_call_target="InvertDiagBlocksLowerTriangular" | custom-call | tf_op jit(solution)/shard_map/first_panel/jit(_solve_triangular)/triangular_solve | solution.py:20
  412.7 11.7 %cholesky.358 = f32[128,128]{1,0:T(8,128)S(1)} custom-call(f32[128,128]{1,0:T(8,128)S(1)} %cholesky.439), custom_call_target="Cholesky" | custom-call | tf_op jit(solution)/shard_map/second_panel/jit(cholesky)/cholesky | solution.py:24
  424.5 9.8 %custom-call.36 = f32[1,128,128]{1,2,0:T(8,128)S(1)} custom-call(f32[1,128,128]{2,1,0:T(8,128)S(1)} %get-tuple-element.121), custom_call_target="InvertDiagBlocksLowerTriangular" | custom-call | tf_op jit(solution)/shard_map/second_panel/jit(cholesky)/cholesky | solution.py:24
  435.0 11.7 %cholesky.377 = f32[128,128]{1,0:T(8,128)S(1)} custom-call(f32[128,128]{1,0:T(8,128)S(1)} %cholesky.443), custom_call_target="Cholesky" | custom-call | tf_op jit(solution)/shard_map/second_panel/jit(cholesky)/cholesky | solution.py:24
  448.1 10.0 %custom-call.37 = f32[1,128,128]{1,2,0:T(8,128)S(1)} custom-call(f32[1,128,128]{2,1,0:T(8,128)S(1)} %get-tuple-element.118), custom_call_target="InvertDiagBlocksLowerTriangular" | custom-call | tf_op jit(solution)/shard_map/second_panel/jit(cholesky)/cholesky | solution.py:24
  458.8 11.7 %cholesky.398 = f32[128,128]{1,0:T(8,128)S(1)} custom-call(f32[128,128]{1,0:T(8,128)S(1)} %cholesky.448), custom_call_target="Cholesky" | custom-call | tf_op jit(solution)/shard_map/second_panel/jit(cholesky)/cholesky | solution.py:24
  471.2 9.8 %custom-call.38 = f32[1,128,128]{1,2,0:T(8,128)S(1)} custom-call(f32[1,128,128]{2,1,0:T(8,128)S(1)} %get-tuple-element.115), custom_call_target="InvertDiagBlocksLowerTriangular" | custom-call | tf_op jit(solution)/shard_map/second_panel/jit(cholesky)/cholesky | solution.py:24
  481.6 11.9 %cholesky.415 = f32[128,128]{1,0:T(8,128)S(1)} custom-call(f32[128,128]{1,0:T(8,128)S(1)} %convolution_subtract_fusion.15), custom_call_target="Cholesky" | custom-call | tf_op jit(solution)/shard_map/second_panel/jit(cholesky)/cholesky | solution.py:24
  498.1 8.1 %while.8 = (s32[]{:T(128)}, f32[512,512]{1,0:T(8,128)S(1)}, s32[4,2]{0,1:T(2,128)S(1)}, f32[4,128,128]{2,1,0:T(8,128)S(1)}, s32[]{:T(128)}) while((s32[]{:T(128)}, f32[512,512]{1,0:T(8,128)S(1)}, s32[4,2]{0,1:T(2,128)S(1)}, f32[4,128,128]{2,1,0:T(8,128)S(1)}, s32[]{:T(128)}) %tuple.83), condition=%wide.while_cond.6, body=%wide.while_body.6.sunk | while | flops 2 | bytes 131181 | solution.py:20
  506.2 39.3 %custom-call.29 = f32[4,128,128]{1,2,0:T(8,128)S(1)} custom-call(f32[4,128,128]{2,1,0:T(8,128)S(1)} %get-tuple-element.81), custom_call_target="InvertDiagBlocksLowerTriangular" | custom-call | tf_op jit(solution)/shard_map/second_panel/jit(_solve_triangular)/triangular_solve | solution.py:20
  (156 shorter events, 97.5 us)
Async XLA Ops:
  6.5 206.0 %all-gather.6.cloned.1.call-start = ((), (), s32[]{:S(2)}) async-start(), calls=%async_computation | async-start | bytes 3151872 | tf_op jit(solution)/shard_map/gather_inputs/all_gather | solution.py:39
  386.5 3.6 copy-start.1
  390.1 1.3 copy-start.7
  399.7 1.2 copy-start.2
  399.7 2.6 copy-start.4
  400.9 2.6 copy-start
  496.8 48.8 %copy-start.3 = (f32[448,512]{1,0:T(8,128)S(1)}, f32[448,512]{1,0:T(8,128)}, u32[]{:S(2)}) copy-start(f32[448,512]{1,0:T(8,128)} %convolution_subtract_fusion.4) | copy-start | bytes 2752516
  496.8 48.8 %copy-start.5 = (f32[224,512]{1,0:T(8,128)S(1)}, f32[224,512]{1,0:T(8,128)}, u32[]{:S(2)}) copy-start(f32[224,512]{1,0:T(8,128)} %convolution_subtract_fusion.7) | copy-start | bytes 1376260
  549.6 1.0 copy-start.6
  550.6 1.0 slice-start
Sparse Core Ops, SparseCore 0:
  11.8 200.7 all-gather.5
